TPU v7x, 256 devices: a whole 4x4x8 slice. The times are simulated.
256 devices in a mesh: dp: 4 (over z_hi), expert: 64 (over y, x, z_lo, core).
Axes of the slice: x: 4, y: 4, z: 8 (z_hi: 4, z_lo: 2; z = z_hi * 2 + z_lo), core: 2. Of those that a mesh axis runs over, the one named last changes fastest.
Arguments:
- tokens: bfloat16 [32768, 3584], P(('dp', 'expert')), may hold values from -6 to 6
- cotangent: bfloat16 [32768, 1024], P(('dp', 'expert')), may hold values from -6 to 6
- expert_ids: int32 [32768, 8], P(('dp', 'expert')), may hold values from 0 to 255, all different within a row; in each aligned block of 128 rows (0 to 127, 128 to 255, ...) at most 6 rows name the same one
- gate_values: float32 [32768, 8], P(('dp', 'expert')), may hold values from 0.1 to 1
- counts: int32 [256], P(('dp', 'expert')), may hold values from 64 to 128
- swap_flags: int32 [64], replicated, may hold values from 0 to 1, as said below
- weights: bfloat16 [64, 3584, 1024], P('expert', 'dp'), may hold values from -0.035888672 to 0.035888672
- first_moment: bfloat16 [64, 3584, 1024], P('expert', 'dp'), may hold values from -6 to 6
- second_moment: bfloat16 [64, 3584, 1024], P('expert', 'dp'), may hold values from 1 to 100
Outputs:
- new_weights: bfloat16 [64, 3584, 1024], P('expert', 'dp')
- new_first: bfloat16 [64, 3584, 1024], P('expert', 'dp')
- new_second: bfloat16 [64, 3584, 1024], P('expert', 'dp')
Inputs may be any that keep to these rules, and one draw needn't show every extreme that they name: `expert_ids`: within the 128 rows of one device no expert is named by more than 6 rows; a token names 8 different experts. swap_flags[e] equals swap_flags[(e + 32) mod 64].
All inputs are finite; a program needn't handle non-finite values.
Results may differ from a plain program's by a relative error of at most 0.015.
Values may be sent and summed in bfloat16 or wider, within the bound.
A program may use at most 128 MiB of HBM per device.

v0:
```python
import jax
import jax.numpy as jnp
from jax import lax
from jax.sharding import PartitionSpec as P

beta_first = 0.9
beta_second = 0.95
bias_first = 1.0 - 0.9**3
bias_second = 1.0 - 0.95**3
learn_rate = 0.005
epsilon = 1e-08


def partner(block, axis, distance):
    count = lax.axis_size(axis)
    route = []
    for low in range(count):
        high = low | 1 << distance
        if high != low and high < count:
            route += [(low, high), (high, low)]
    return lax.ppermute(block, axis, route)


def slope_of(preact, gate_rows, cot_rows):
    sigm = jax.nn.sigmoid(preact)
    return (
        gate_rows[:, None] * cot_rows.astype(jnp.float32) * sigm * (1.0 + preact * (1.0 - sigm))
    ).astype(jnp.bfloat16)


def adam_step(weight, first, second, grad):
    first_new = beta_first * first.astype(jnp.float32) + (1.0 - beta_first) * grad
    second_new = beta_second * second.astype(jnp.float32) + (1.0 - beta_second) * grad * grad
    ratio = first_new / bias_first / (jnp.sqrt(second_new / bias_second) + epsilon)
    wfull = weight.astype(jnp.float32)
    updated = (wfull - learn_rate * ratio).astype(jnp.bfloat16)
    return (updated, first_new.astype(jnp.bfloat16), second_new.astype(jnp.bfloat16))


def shards(
    tokens,
    cotangent,
    expert_ids,
    gate_values,
    counts,
    swap_flags,
    weights,
    first_moment,
    second_moment,
):
    experts = lax.axis_size("expert")
    half_axis = experts // 2
    partner_bit = experts.bit_length() - 2
    tok_rows = tokens.shape[0]
    top_count = expert_ids.shape[1]
    most_slots = min(tok_rows, tok_rows * top_count * 3 // (8 * experts))
    slot_rows = experts * most_slots
    lanes = jnp.arange(experts, dtype=jnp.int32)
    own_flag = jnp.sum(jnp.where(lanes == lax.axis_index("expert"), swap_flags, 0))
    stacked = jnp.concatenate([weights, first_moment, second_moment], axis=0)
    moved = partner(stacked, "expert", partner_bit)
    settled = jnp.where(own_flag == 1, moved, stacked)
    weight_here = settled[0]
    live = jnp.arange(tok_rows, dtype=jnp.int32) < counts[0]
    named = (expert_ids[:, :, None] == lanes).astype(jnp.int32)
    flagged = jnp.sum(named * swap_flags, axis=2)
    target = jnp.where(flagged == 1, (expert_ids + half_axis) % experts, expert_ids)
    landed = ((target[:, :, None] == lanes) & live[:, None, None]).astype(jnp.int32)
    landed = landed.reshape(tok_rows * top_count, experts)
    ranked = jnp.cumsum(landed, axis=0) - landed
    places = jnp.sum(ranked * landed, axis=1).reshape(tok_rows, top_count)
    slot_hits = (places[:, :, None] == jnp.arange(most_slots, dtype=jnp.int32)).astype(jnp.float32)
    landing = landed.reshape(tok_rows, top_count, experts).astype(jnp.float32)
    picker = jnp.einsum("tkn,tks->nst", landing, slot_hits, precision=lax.Precision.HIGHEST)
    picker = picker.reshape(slot_rows, tok_rows).astype(jnp.bfloat16)
    gate_slots = jnp.einsum(
        "tkn,tks,tk->ns", landing, slot_hits, gate_values, precision=lax.Precision.HIGHEST
    )
    feature_slots = jnp.dot(picker, tokens, preferred_element_type=jnp.float32).astype(jnp.bfloat16)
    feature_slots = feature_slots.reshape(experts, most_slots, tokens.shape[1])
    cot_slots = jnp.dot(picker, cotangent, preferred_element_type=jnp.float32).astype(jnp.bfloat16)
    cot_slots = cot_slots.reshape(experts, most_slots, cotangent.shape[1])
    arrived = (
        lax.all_to_all(feature_slots, "expert", split_axis=0, concat_axis=0, tiled=True),
        lax.all_to_all(cot_slots, "expert", split_axis=0, concat_axis=0, tiled=True),
        lax.all_to_all(
            gate_slots.astype(jnp.bfloat16), "expert", split_axis=0, concat_axis=0, tiled=True
        ).astype(gate_slots.dtype),
    )
    row_feat = arrived[0].reshape(slot_rows, tokens.shape[1])
    row_cot = arrived[1].reshape(slot_rows, cotangent.shape[1])
    row_gate = arrived[2].reshape(slot_rows)
    columns = row_feat
    preact = jnp.dot(
        columns,
        lax.all_gather(weight_here, "dp", axis=0, tiled=True),
        preferred_element_type=jnp.float32,
    )
    slope = slope_of(preact, row_gate, row_cot)
    columns = row_feat
    grad = lax.psum_scatter(
        lax.dot_general(
            columns, slope, (((0,), (0,)), ((), ())), preferred_element_type=jnp.float32
        ).astype(jnp.bfloat16),
        "dp",
        scatter_dimension=0,
        tiled=True,
    ).astype(jnp.float32)
    first_here = settled[1]
    second_here = settled[2]
    updated, first_new, second_new = adam_step(weight_here, first_here, second_here, grad)
    return (updated[None], first_new[None], second_new[None])


def solution(mesh):
    placed = (
        P(("dp", "expert"), None),
        P(("dp", "expert"), None),
        P(("dp", "expert"), None),
        P(("dp", "expert"), None),
        P(("dp", "expert")),
        P(),
        P("expert", "dp", None),
        P("expert", "dp", None),
        P("expert", "dp", None),
    )
    return jax.shard_map(
        shards,
        mesh=mesh,
        in_specs=placed,
        out_specs=(P("expert", "dp", None), P("expert", "dp", None), P("expert", "dp", None)),
        check_vma=False,
    )
```

profile of v0, /device:TPU:5, one launch (start us, length us, event | category | flops | bytes accessed | tf_op | source)
XLA Modules:
  0.0 501.2 jit_solution(18124079884895477463)
XLA Ops:
  7.2 0.0 copy-start
  7.2 0.0 copy-start.4
  7.2 0.0 all-gather.3.cloned.1.call-start
  7.2 0.0 copy-start.5
  7.2 3.1 constant_dynamic-update-slice_fusion.2
  10.3 0.0 copy-done.4
  10.3 1.4 constant_dynamic-update-slice_fusion.1
  11.7 0.0 copy-done.5
  11.7 1.4 constant_dynamic-update-slice_fusion
  13.1 2.9 collective-permute-start
  16.0 0.0 copy-done.8
  16.0 0.6 fusion.28
  17.3 117.1 %collective-permute-done = bf16[3,896,1024]{2,1,0:T(8,128)(2,1)} collective-permute-done((bf16[3,896,1024]{2,1,0:T(8,128)(2,1)}, bf16[3,896,1024]{2,1,0:T(8,128)(2,1)}, u32[]{:S(2)}, u32[]{:S(2)}) %collective-permute-start) | collective-permute-done | bytes 5505056 | tf_op jit(solution)/shard_map/ppermute | solution.py:21
  134.4 3.1 broadcast_select_fusion
  137.6 0.0 copy-start.2
  137.6 2.4 copy-done.2
  139.9 1.4 slice.20
  141.3 0.0 all-gather.3.cloned.1.call-update
  141.3 0.0 copy-done.7
  141.3 0.1 select_reduce_fusion
  141.5 0.1 copy.35
  141.6 0.1 eq.89
  141.7 0.1 eq.85
  142.4 0.1 and.38
  142.5 0.1 and.39
  142.6 0.1 and.34
  142.7 0.1 and.35
  142.8 18.0 %reduce-window.6 = s32[64,8,128]{2,1,0:T(8,128)S(1)} reduce-window(s32[64,8,128]{2,1,0:T(8,128)S(1)} %fusion.20, s32[]{:T(128)} %constant.18.clone.1), window={size=1x1x128 pad=0_0x0_0x127_0}, to_apply=%region_2.3 | reduce-window | flops 8323072 | bytes 524292 | tf_op jit(solution)/shard_map/reduce-window
  160.9 0.1 slice.22
  161.0 0.1 copy.37
  161.2 0.1 copy.38
  161.3 0.1 broadcast_add_fusion
  161.4 0.1 fusion.17
  161.5 0.1 eq.93
  161.6 0.0 copy-done.9
  161.6 0.3 fusion.14
  162.0 0.8 copy.43
  162.8 10.5 %all-to-all-start.1 = ((bf16[64,1,6]{2,1,0:T(2,128)(2,1)}), bf16[64,1,6]{2,1,0:T(2,128)(2,1)S(1)}, u32[]{:S(2)}, u32[]{:S(2)}) async-start(bf16[64,1,6]{2,1,0:T(2,128)(2,1)} %copy.43), calls=%async_computation.1 | async-start | bytes 65536 | tf_op jit(solution)/shard_map/all_to_all | solution.py:86
  173.3 0.3 copy.40
  173.6 0.2 copy.41
  173.9 0.6 fusion.12
  174.4 0.2 copy.42
  174.7 0.0 copy-done.6
  174.7 0.4 convolution_convert_fusion.2
  175.1 1.2 reshape.72
  176.3 2.9 all-to-all-done.1
  179.2 6.8 %all-to-all-start.2 = ((bf16[64,6,1024]{2,1,0:T(8,128)(2,1)}), bf16[64,6,1024]{2,1,0:T(8,128)(2,1)S(1)}, u32[]{:S(2)}, u32[]{:S(2)}) async-start(bf16[64,6,1024]{2,1,0:T(8,128)(2,1)} %reshape.72), calls=%async_computation.2 | async-start | bytes 2097152 | tf_op jit(solution)/shard_map/all_to_all | solution.py:85
  186.0 0.0 copy-done
  186.0 2.4 convolution_convert_fusion.1
  188.4 5.4 %reshape.70 = bf16[64,6,3584]{2,1,0:T(8,128)(2,1)} reshape(bf16[384,3584]{1,0:T(8,128)(2,1)} %convolution_convert_fusion.1) | data formatting | bytes 5505024 | tf_op jit(solution)/shard_map/reshape | solution.py:80
  193.8 47.5 %all-to-all-done.2 = bf16[64,6,1024]{2,1,0:T(8,128)(2,1)S(1)} async-done(((bf16[64,6,1024]{2,1,0:T(8,128)(2,1)}), bf16[64,6,1024]{2,1,0:T(8,128)(2,1)S(1)}, u32[]{:S(2)}, u32[]{:S(2)}) %all-to-all-start.2) | async-done | bytes 786464 | tf_op jit(solution)/shard_map/all_to_all | solution.py:85
  241.3 13.6 %all-to-all-start = ((bf16[64,6,3584]{2,1,0:T(8,128)(2,1)}), bf16[64,6,3584]{2,1,0:T(8,128)(2,1)}, u32[]{:S(2)}, u32[]{:S(2)}) async-start(bf16[64,6,3584]{2,1,0:T(8,128)(2,1)} %reshape.70), calls=%async_computation | async-start | bytes 7340032 | tf_op jit(solution)/shard_map/all_to_all | solution.py:84
  254.9 0.2 reduce-scatter.2.cloned.1.call-start
  255.1 0.1 convert_reduce_fusion
  255.2 0.1 reshape.73
  255.4 0.2 reshape.74
  255.6 78.5 %all-to-all-done = bf16[64,6,3584]{2,1,0:T(8,128)(2,1)} async-done(((bf16[64,6,3584]{2,1,0:T(8,128)(2,1)}), bf16[64,6,3584]{2,1,0:T(8,128)(2,1)}, u32[]{:S(2)}, u32[]{:S(2)}) %all-to-all-start) | async-done | bytes 2752544 | tf_op jit(solution)/shard_map/all_to_all | solution.py:84
  334.1 5.5 %reshape.71 = bf16[384,3584]{1,0:T(8,128)(2,1)} reshape(bf16[64,6,3584]{2,1,0:T(8,128)(2,1)} %all-to-all-done) | data formatting | bytes 5505024 | tf_op jit(solution)/shard_map/reshape | solution.py:90
  339.5 7.4 %multiply_convert_fusion = bf16[384,1024]{1,0:T(8,128)(2,1)S(1)} fusion(f32[384,1024]{1,0:T(8,128)S(1)} %reshape.74, bf16[384,3584]{1,0:T(8,128)(2,1)} %reshape.71, bf16[1,3584,1024]{2,1,0:T(8,128)(2,1)} %all-gather.3.cloned.1.call-done, f32[384]{0:T(512)S(1)} %reshape.73), kind=kOutput, calls=%fused_computation.16 | convolution fusion | flops 2822504448 | bytes 12453376 | tf_op jit(solution)/shard_map/dot_general | solution.py:94
  347.0 6.1 %convolution_convert_fusion = bf16[3584,1024]{1,0:T(8,128)(2,1)} fusion(bf16[384,3584]{1,0:T(8,128)(2,1)S(1)} %copy-done.3, bf16[384,1024]{1,0:T(8,128)(2,1)S(1)} %multiply_convert_fusion), kind=kOutput, calls=%fused_computation | convolution fusion | flops 2822242304 | bytes 10878976 | tf_op jit(solution)/shard_map/dot_general | solution.py:102
  353.1 0.0 reduce-scatter.2.cloned.1.call-update
  353.1 0.0 copy-start.1
  353.1 134.4 %reduce-scatter.2.cloned.1.call-done = bf16[896,1024]{1,0:T(8,128)(2,1)} async-done(((bf16[3584,1024]{1,0:T(8,128)(2,1)}), bf16[896,1024]{1,0:T(8,128)(2,1)}) %reduce-scatter.2.cloned.1.call-update) | async-done | bytes 1835024 | tf_op jit(solution)/shard_map/reduce_scatter | solution.py:101
  487.5 6.9 %fusion.7 = (bf16[1,896,1024]{2,1,0:T(8,128)(2,1)}, bf16[1,896,1024]{2,1,0:T(8,128)(2,1)}, bf16[1,896,1024]{2,1,0:T(8,128)(2,1)}) fusion(bf16[896,1024]{1,0:T(8,128)(2,1)} %reduce-scatter.2.cloned.1.call-done, bf16[3,896,1024]{2,1,0:T(8,128)(2,1)} %copy-done.2), kind=kLoop, calls=%fused_computation.13 | loop fusion | flops 18350080 | bytes 12845056 | tf_op jit(solution)/shard_map/broadcast_in_dim | solution.py:112
  (18 shorter events, 0.2 us)
Async XLA Ops:
  7.2 178.9 %copy-start = (bf16[128,3584]{1,0:T(8,128)(2,1)S(1)}, bf16[128,3584]{1,0:T(8,128)(2,1)}, u32[]{:S(2)}) copy-start(bf16[128,3584]{1,0:T(8,128)(2,1)} %param.9) | copy-start | bytes 2752516
  7.2 3.1 copy-start.4
  7.2 332.3 %all-gather.3.cloned.1.call-start = ((), (), s32[]{:S(2)}) async-start(), calls=%async_computation.5 | async-start | bytes 9175040 | tf_op jit(solution)/shard_map/all_gather | solution.py:96
  7.2 4.4 copy-start.5
  10.3 5.7 %copy-start.8 = (s32[64]{0:T(128)S(1)}, s32[64]{0:T(128)}, u32[]{:S(2)}) copy-start(s32[64]{0:T(128)} %param.14) | copy-start | bytes 772
  13.1 121.3 %collective-permute-start = (bf16[3,896,1024]{2,1,0:T(8,128)(2,1)}, bf16[3,896,1024]{2,1,0:T(8,128)(2,1)}, u32[]{:S(2)}, u32[]{:S(2)}) collective-permute-start(bf16[3,896,1024]{2,1,0:T(8,128)(2,1)} %constant_dynamic-update-slice_fusion), channel_id=1, source_target_pairs={{0,32},{32,0},{1,33},{33,1},{2,34},{34,2},{3,35},{35,3},{4,36},{36... | collective-permute-start | bytes 16515080 | tf_op jit(solution)/shard_map/ppermute | solution.py:21
  137.6 2.4 copy-start.2
  139.9 1.4 copy-start.7
  139.9 21.7 %copy-start.9 = (f32[128,8]{0,1:T(8,128)S(1)}, f32[128,8]{0,1:T(8,128)}, u32[]{:S(2)}) copy-start(f32[128,8]{0,1:T(8,128)} %param.12) | copy-start | bytes 12292
  141.3 33.4 %copy-start.6 = (bf16[128,1024]{1,0:T(8,128)(2,1)S(1)}, bf16[128,1024]{1,0:T(8,128)(2,1)}, u32[]{:S(2)}) copy-start(bf16[128,1024]{1,0:T(8,128)(2,1)} %param.10) | copy-start | bytes 786436
  162.8 16.4 %all-to-all-start.1 = ((bf16[64,1,6]{2,1,0:T(2,128)(2,1)}), bf16[64,1,6]{2,1,0:T(2,128)(2,1)S(1)}, u32[]{:S(2)}, u32[]{:S(2)}) async-start(bf16[64,1,6]{2,1,0:T(2,128)(2,1)} %copy.43), calls=%async_computation.1 | async-start | bytes 65536 | tf_op jit(solution)/shard_map/all_to_all | solution.py:86
  179.2 62.1 %all-to-all-start.2 = ((bf16[64,6,1024]{2,1,0:T(8,128)(2,1)}), bf16[64,6,1024]{2,1,0:T(8,128)(2,1)S(1)}, u32[]{:S(2)}, u32[]{:S(2)}) async-start(bf16[64,6,1024]{2,1,0:T(8,128)(2,1)} %reshape.72), calls=%async_computation.2 | async-start | bytes 2097152 | tf_op jit(solution)/shard_map/all_to_all | solution.py:85
  241.3 92.8 %all-to-all-start = ((bf16[64,6,3584]{2,1,0:T(8,128)(2,1)}), bf16[64,6,3584]{2,1,0:T(8,128)(2,1)}, u32[]{:S(2)}, u32[]{:S(2)}) async-start(bf16[64,6,3584]{2,1,0:T(8,128)(2,1)} %reshape.70), calls=%async_computation | async-start | bytes 7340032 | tf_op jit(solution)/shard_map/all_to_all | solution.py:84
  254.9 232.6 %reduce-scatter.2.cloned.1.call-start = ((), (), s32[]{:S(2)}) async-start(), calls=%async_computation.4 | async-start | bytes 9175040 | tf_op jit(solution)/shard_map/reduce_scatter | solution.py:101
  339.5 7.4 %copy-start.3 = (bf16[384,3584]{1,0:T(8,128)(2,1)S(1)}, bf16[384,3584]{1,0:T(8,128)(2,1)}, u32[]{:S(2)}) copy-start(bf16[384,3584]{1,0:T(8,128)(2,1)} %reshape.71) | copy-start | bytes 8257540
  353.1 141.3 %copy-start.1 = (bf16[128,3584]{1,0:T(8,128)(2,1)S(1)}, bf16[128,3584]{1,0:T(8,128)(2,1)}, u32[]{:S(2)}) copy-start(bf16[128,3584]{1,0:T(8,128)(2,1)} %param.9) | copy-start | bytes 2752516
Sparse Core Ops, SparseCore 0:
  141.4 179.5 all-gather.2
  353.2 134.2 reduce-scatter.1
where the time goes:
time: 502 us; the launch traced here: 501 us
  waiting for transfers between devices  380 us (76%)
  starting transfers between devices  34.1 us (7%)
  other arithmetic  29.2 us (6%)
  local copies, waits for them, and re-layouts  24.7 us (5%)
  matrix products  17.2 us (3%)
  between operations  15.6 us (3%)
    reduce_scatter x1, waiting for transfers between devices, shards(): lax.psum_scatter(lax.dot_general(columns, slope, (((0,), (0,)), ((), ()))...  134 us
    ppermute x1, waiting for transfers between devices, partner(): return lax.ppermute(block, axis, route)  117 us
    all_to_all x1, waiting for transfers between devices, shards(): lax.all_to_all(feature_slots, 'expert', split_axis=0, concat_axis=0, tile...  78.5 us
    all_to_all x1, waiting for transfers between devices, shards(): lax.all_to_all(cot_slots, 'expert', split_axis=0, concat_axis=0, tiled=True)  47.5 us
    another operation x3, other arithmetic  18.2 us
    all_to_all x1, starting transfers between devices, shards(): lax.all_to_all(feature_slots, 'expert', split_axis=0, concat_axis=0, tile...  13.6 us
    all_to_all x1, starting transfers between devices, shards(): lax.all_to_all(gate_slots.astype(jnp.bfloat16), 'expert', split_axis=0, c...  10.5 us
  transfers between devices with their start and end apart: 6, of which 5 were waited for; matrix products, arithmetic and copies ran while one was open for 8% of the time, Pallas kernels for 0%

commit v1 on v0

v1 whole, which is shorter than its diff:
```python
import jax
import jax.numpy as jnp
from jax import lax
from jax.sharding import PartitionSpec as P

beta_first = 0.9
beta_second = 0.95
bias_first = 1.0 - 0.9**3
bias_second = 1.0 - 0.95**3
learn_rate = 0.005
epsilon = 1e-08
most = 6
aux_cols = 128


def partner(block, axis, distance):
    count = lax.axis_size(axis)
    route = [(low, low ^ (1 << distance)) for low in range(count)]
    return lax.ppermute(block, axis, route)


def adam_step(weight, first, second, grad):
    first_new = beta_first * first.astype(jnp.float32) + (1.0 - beta_first) * grad
    second_new = beta_second * second.astype(jnp.float32) + (1.0 - beta_second) * grad * grad
    ratio = first_new / bias_first / (jnp.sqrt(second_new / bias_second) + epsilon)
    wfull = weight.astype(jnp.float32)
    updated = (wfull - learn_rate * ratio).astype(jnp.bfloat16)
    return (updated, first_new.astype(jnp.bfloat16), second_new.astype(jnp.bfloat16))


def routing(expert_ids, gate_values, counts, swap_flags, experts):
    tok_rows, top = expert_ids.shape
    lanes = jnp.arange(experts, dtype=jnp.int32)
    live = jnp.arange(tok_rows, dtype=jnp.int32)[:, None] < counts[0]
    named = [(expert_ids[:, k : k + 1] == lanes) & live for k in range(top)]
    every = sum(n.astype(jnp.float32) for n in named)
    earlier = jnp.tril(jnp.ones((tok_rows, tok_rows), jnp.bfloat16), -1)
    ranked = jnp.dot(earlier, every.astype(jnp.bfloat16), preferred_element_type=jnp.float32)
    half = experts // 2
    slot_of = jnp.where(swap_flags == 1, (lanes + half) % experts, lanes).astype(jnp.float32)
    target = jnp.stack([jnp.sum(jnp.where(n, slot_of + 1.0, 0.0), axis=1) for n in named], axis=1) - 1.0
    place = jnp.stack([jnp.sum(jnp.where(n, ranked, 0.0), axis=1) for n in named], axis=1)
    aux = jnp.concatenate([target, place, gate_values], axis=1)
    aux = jnp.pad(aux, ((0, 0), (0, aux_cols - 3 * top)))
    return aux.astype(jnp.bfloat16)


def shards(tokens, cotangent, expert_ids, gate_values, counts, swap_flags, weights, first_moment, second_moment):
    experts = lax.axis_size("expert")
    groups = lax.axis_size("dp")
    partner_bit = experts.bit_length() - 2
    tok_rows, width = tokens.shape
    hidden = cotangent.shape[1]
    top = expert_ids.shape[1]
    dpart, fpart = width // groups, hidden // groups
    lanes = jnp.arange(experts, dtype=jnp.int32)
    own_flag = jnp.sum(jnp.where(lanes == lax.axis_index("expert"), swap_flags, 0))

    moved_w = partner(weights, "expert", partner_bit)
    aux = routing(expert_ids, gate_values, counts, swap_flags, experts)
    blocks = jnp.stack(
        [
            jnp.concatenate(
                [tokens[:, r * dpart : (r + 1) * dpart], cotangent[:, r * fpart : (r + 1) * fpart], aux], axis=1
            )
            for r in range(groups)
        ]
    )
    recv = lax.all_to_all(blocks, "dp", split_axis=0, concat_axis=0, tiled=True)
    recv_rows = groups * tok_rows
    recv = recv.reshape(recv_rows, dpart + fpart + aux_cols)
    info = recv[:, dpart + fpart : dpart + fpart + 3 * top].astype(jnp.float32).T
    per_slot = groups * most
    group_base = (jnp.arange(recv_rows) // tok_rows * most).astype(jnp.float32)
    code = jnp.where(info[:top] >= 0, info[:top] * per_slot + info[top : 2 * top] + group_base, -1.0)
    gates = info[2 * top :]
    slots = lax.broadcasted_iota(jnp.int32, (experts * per_slot, recv_rows), 0).astype(jnp.float32)
    picker = jnp.zeros(slots.shape, jnp.float32)
    gated = jnp.zeros(slots.shape, jnp.float32)
    for k in range(top):
        hit = slots == code[k][None, :]
        picker = jnp.where(hit, 1.0, picker)
        gated = jnp.where(hit, gates[k][None, :], gated)
    xs = jnp.dot(picker.astype(jnp.bfloat16), recv[:, :dpart], preferred_element_type=jnp.float32)
    cs = jnp.dot(gated.astype(jnp.bfloat16), recv[:, dpart : dpart + fpart], preferred_element_type=jnp.float32)
    send = jnp.concatenate([xs.astype(jnp.bfloat16), cs.astype(jnp.bfloat16)], axis=1)
    send = send.reshape(experts, per_slot, dpart + fpart)
    got = lax.all_to_all(send, "expert", split_axis=0, concat_axis=0, tiled=True)
    got = got.reshape(experts * per_slot, dpart + fpart)
    x = got[:, :dpart]
    c = got[:, dpart:]

    moved_m = partner(first_moment, "expert", partner_bit)
    moved_v = partner(second_moment, "expert", partner_bit)
    weight = jnp.where(own_flag == 1, moved_w, weights)[0]
    zpart = jnp.stack(
        [
            jnp.dot(x, weight[:, r * fpart : (r + 1) * fpart], preferred_element_type=jnp.float32).astype(jnp.bfloat16)
            for r in range(groups)
        ]
    )
    z = lax.psum_scatter(zpart, "dp", scatter_dimension=0, tiled=False).astype(jnp.float32)
    sigm = jax.nn.sigmoid(z)
    slope = (c.astype(jnp.float32) * sigm * (1.0 + z * (1.0 - sigm))).astype(jnp.bfloat16)
    slopes = lax.all_gather(slope, "dp", axis=0, tiled=False)
    grad = jnp.concatenate(
        [
            lax.dot_general(x, slopes[r], (((0,), (0,)), ((), ())), preferred_element_type=jnp.float32)
            for r in range(groups)
        ],
        axis=1,
    )
    first = jnp.where(own_flag == 1, moved_m, first_moment)[0]
    second = jnp.where(own_flag == 1, moved_v, second_moment)[0]
    updated, first_new, second_new = adam_step(weight, first, second, grad)
    return (updated[None], first_new[None], second_new[None])


def solution(mesh):
    placed = (
        P(("dp", "expert"), None),
        P(("dp", "expert"), None),
        P(("dp", "expert"), None),
        P(("dp", "expert"), None),
        P(("dp", "expert")),
        P(),
        P("expert", "dp", None),
        P("expert", "dp", None),
        P("expert", "dp", None),
    )
    return jax.shard_map(
        shards,
        mesh=mesh,
        in_specs=placed,
        out_specs=(P("expert", "dp", None), P("expert", "dp", None), P("expert", "dp", None)),
        check_vma=False,
    )
```

time: 502 us -> 354 us (0.71)
  waiting for transfers between devices: 380 us -> 231 us
  matrix products: 17.2 us -> 29.2 us
  other arithmetic: 29.2 us -> 20.4 us
  starting transfers between devices: 34.1 us -> 28.6 us
    all_to_all x3 -> x2, waiting for transfers between devices: 129 us -> 28.7 us  [the longest x1 28.7 us: shards(): recv = lax.all_to_all(blocks, 'dp', split_axis=0, concat_axis=0, tiled=True)]
    reduce_scatter x1, waiting for transfers between devices: 134 us -> 64.9 us  [shards(): lax.psum_scatter(zpart, 'dp', scatter_dimension=0, tiled=False)]
    all_gather x1, waiting for transfers between devices: 0.01 us -> 50.8 us  [shards(): slopes = lax.all_gather(slope, 'dp', axis=0, tiled=False)]
    ppermute x1 -> x3, waiting for transfers between devices: 117 us -> 86.6 us  [partner(): return lax.ppermute(block, axis, route)]
    another operation x3 -> x5, other arithmetic: 18.2 us -> 3.91 us  [the longest x1 1.89 us: shards(): jnp.stack([jnp.dot(x, weight[:, r * fpart:(r + 1) * fpart], preferred_ele...]
    unnamed x22, local copies, waits for them, and re-layouts: 6.83 us -> 21 us
    reshape x3 -> x0, local copies, waits for them, and re-layouts: 12.1 us -> none  [the longest x1 5.46 us: shards(): row_feat = arrived[0].reshape(slot_rows, tokens.shape[1])]
    dot_general x6 -> x11, matrix products: 17.2 us -> 29.2 us  [the longest x4 11.7 us: shards(): lax.dot_general(x, slopes[r], (((0,), (0,)), ((), ())), preferred_element...]
  transfers between devices with their start and end apart: 6 -> 7, of which waited for: 5 -> 5; matrix products, arithmetic and copies ran while one was open for 8% -> 7% of each run, Pallas kernels for 0% -> 0%
where the time goes in v1:
time: 354 us; the launch traced here: 352 us
  waiting for transfers between devices  231 us (65%)
  matrix products  29.2 us (8%)
  starting transfers between devices  28.6 us (8%)
  local copies, waits for them, and re-layouts  27.3 us (8%)
  other arithmetic  20.4 us (6%)
  between operations  15.6 us (4%)
    ppermute x3, waiting for transfers between devices, partner(): return lax.ppermute(block, axis, route)  86.6 us
    reduce_scatter x1, waiting for transfers between devices, shards(): lax.psum_scatter(zpart, 'dp', scatter_dimension=0, tiled=False)  64.9 us
    all_gather x1, waiting for transfers between devices, shards(): slopes = lax.all_gather(slope, 'dp', axis=0, tiled=False)  50.8 us
    all_to_all x1, waiting for transfers between devices, shards(): recv = lax.all_to_all(blocks, 'dp', split_axis=0, concat_axis=0, tiled=True)  28.7 us
    unnamed x22, local copies, waits for them, and re-layouts  21 us
    all_to_all x1, starting transfers between devices, shards(): lax.all_to_all(send, 'expert', split_axis=0, concat_axis=0, tiled=True)  14.4 us
    dot_general x4, matrix products, shards(): lax.dot_general(x, slopes[r], (((0,), (0,)), ((), ())), preferred_element...  11.7 us
    dot_general x4, matrix products, shards(): jnp.dot(x, weight[:, r * fpart:(r + 1) * fpart], preferred_element_type=j...  11.4 us
  transfers between devices with their start and end apart: 7, of which 5 were waited for; matrix products, arithmetic and copies ran while one was open for 7% of the time, Pallas kernels for 0%

profile of v1, /device:TPU:5, one launch (start us, length us, event | category | flops | bytes accessed | tf_op | source)
XLA Modules:
  0.0 352.0 jit_solution(3110349488905378927)
XLA Ops:
  7.2 0.0 copy-start.4
  7.2 1.0 slice_bitcast_fusion.7
  8.8 0.7 convert_add_fusion
  9.5 0.3 select_reduce_fusion
  9.8 0.7 convert.51
  10.5 0.1 concatenate.51
  10.5 0.1 copy.42
  10.7 1.4 fusion.111
  12.0 0.0 copy-done.4
  12.1 0.1 fusion.68
  12.2 1.2 pad_maximum_fusion.3
  13.4 8.2 %all-to-all-start = ((bf16[4,128,1280]{2,1,0:T(8,128)(2,1)}), bf16[4,128,1280]{2,1,0:T(8,128)(2,1)S(1)}, u32[]{:S(2)}, u32[]{:S(2)}) async-start(bf16[4,128,1280]{2,1,0:T(8,128)(2,1)} %pad_maximum_fusion.3), calls=%async_computation | async-start | bytes 2621440 | tf_op jit(solution)/shard_map/all_to_all | solution.py:69
  21.6 28.7 %all-to-all-done = bf16[4,128,1280]{2,1,0:T(8,128)(2,1)S(1)} async-done(((bf16[4,128,1280]{2,1,0:T(8,128)(2,1)}), bf16[4,128,1280]{2,1,0:T(8,128)(2,1)S(1)}, u32[]{:S(2)}, u32[]{:S(2)}) %all-to-all-start) | async-done | bytes 1310752 | tf_op jit(solution)/shard_map/all_to_all | solution.py:69
  50.3 0.1 copy.41
  50.5 3.3 convolution_convert_fusion
  53.8 2.6 convolution_convert_fusion.5
  56.4 0.2 pad_maximum_fusion.1
  56.6 3.9 %copy.35 = bf16[1536,1152]{1,0:T(8,128)(2,1)} copy(bf16[1536,1152]{0,1:T(8,128)(2,1)S(1)} %pad_maximum_fusion.1) | data formatting | bytes 7077888 | tf_op jit(solution)/shard_map/concatenate | solution.py:86
  60.5 14.4 %all-to-all-start.1 = ((bf16[64,24,1152]{2,1,0:T(8,128)(2,1)}), bf16[64,24,1152]{2,1,0:T(8,128)(2,1)}, u32[]{:S(2)}, u32[]{:S(2)}) async-start(bf16[64,24,1152]{2,1,0:T(8,128)(2,1)} %bitcast.47), calls=%async_computation.1 | async-start | bytes 7077888 | tf_op jit(solution)/shard_map/all_to_all | solution.py:88
  74.9 0.0 copy-start.6
  74.9 0.0 reduce-scatter.2.cloned.1.call-start
  75.0 3.1 copy.26
  78.0 2.9 collective-permute-start
  81.0 0.0 copy-done.6
  81.0 0.6 fusion.102
  82.3 73.8 %collective-permute-done = bf16[1,896,1024]{1,2,0:T(8,128)(2,1)} collective-permute-done((bf16[1,896,1024]{1,2,0:T(8,128)(2,1)S(1)}, bf16[1,896,1024]{1,2,0:T(8,128)(2,1)}, u32[]{:S(2)}, u32[]{:S(2)}) %collective-permute-start) | collective-permute-done | bytes 1835040 | tf_op jit(solution)/shard_map/ppermute | solution.py:19
  156.0 2.9 fusion.49
  158.9 0.0 all-to-all-done.1
  158.9 0.0 copy-start.3
  158.9 3.0 fusion.3
  161.9 0.0 copy-done.3
  161.9 2.8 fusion.4
  164.7 2.8 fusion.5
  167.5 2.8 fusion.6
  170.3 1.9 pad_maximum_fusion.2
  172.2 0.0 reduce-scatter.2.cloned.1.call-update
  172.2 0.0 all-gather.3.cloned.1.call-start
  172.3 64.9 %reduce-scatter.2.cloned.1.call-done = bf16[1,1536,256]{2,1,0:T(8,128)(2,1)} async-done(((bf16[4,1536,256]{2,1,0:T(8,128)(2,1)}), bf16[1,1536,256]{2,1,0:T(8,128)(2,1)}) %reduce-scatter.2.cloned.1.call-update) | async-done | bytes 786448 | tf_op jit(solution)/shard_map/reduce_scatter | solution.py:102
  237.2 2.9 fusion.14
  240.1 0.0 all-gather.3.cloned.1.call-update
  240.2 3.8 %copy.28 = bf16[1,896,1024]{1,2,0:T(8,128)(2,1)} copy(bf16[1,896,1024]{2,1,0:T(8,128)(2,1)} %param.16) | data formatting | bytes 3670016 | tf_op args[7]
  244.0 2.8 collective-permute-start.1
  246.7 3.8 %copy.36 = bf16[1,896,1024]{1,2,0:T(8,128)(2,1)} copy(bf16[1,896,1024]{2,1,0:T(8,128)(2,1)} %param.17) | data formatting | bytes 3670016 | tf_op args[8]
  250.5 0.2 collective-permute-start.2
  250.7 50.8 %all-gather.3.cloned.1.call-done = bf16[6144,256]{1,0:T(8,128)(2,1)} async-done(((bf16[1536,256]{1,0:T(8,128)(2,1)}), bf16[6144,256]{1,0:T(8,128)(2,1)}) %all-gather.3.cloned.1.call-update) | async-done | bytes 3145744 | tf_op jit(solution)/shard_map/all_gather | solution.py:105
  301.5 0.0 copy-start.5
  301.5 3.1 convolution_bitcast_fusion.3
  304.6 0.0 copy-done.5
  304.6 2.8 convolution_bitcast_fusion.2
  307.4 2.8 convolution_bitcast_fusion.1
  310.3 0.0 copy-start
  310.3 0.0 copy-start.1
  310.3 2.9 convolution_bitcast_fusion
  313.2 0.0 collective-permute-done.1
  313.2 12.8 %collective-permute-done.2 = bf16[1,896,1024]{1,2,0:T(8,128)(2,1)} collective-permute-done((bf16[1,896,1024]{1,2,0:T(8,128)(2,1)}, bf16[1,896,1024]{1,2,0:T(8,128)(2,1)}, u32[]{:S(2)}, u32[]{:S(2)}) %collective-permute-start.2) | collective-permute-done | bytes 1835040 | tf_op jit(solution)/shard_map/ppermute | solution.py:19
  326.0 0.0 copy-done
  326.0 0.0 copy-done.1
  326.0 9.1 %fusion.110 = (bf16[1,896,1024]{1,2,0:T(8,128)(2,1)}, bf16[1,896,1024]{1,2,0:T(8,128)(2,1)}, bf16[1,896,1024]{1,2,0:T(8,128)(2,1)}) fusion(f32[1,896,256]{1,2,0:T(8,128)S(1)} %convolution_bitcast_fusion, f32[1,896,256]{1,2,0:T(8,128)S(1)} %convolution_bitcast_fusion.1, f32[1,896,256]{1,2,0:T(8,128)S(1)} %convolution_bitcast_fusion.2, ...), kind=kLoop, calls=%fused_computation.202 | loop fusion | flops 22937600 | bytes 20185088 | tf_op jit(solution)/shard_map/convert_element_type | solution.py:28
  335.1 3.8 %copy.38 = bf16[1,896,1024]{2,1,0:T(8,128)(2,1)} copy(bf16[1,896,1024]{1,2,0:T(8,128)(2,1)} %get-tuple-element.26) | data formatting | bytes 3670016
  338.9 0.0 copy-start.2
  338.9 3.9 %copy.39 = bf16[1,896,1024]{2,1,0:T(8,128)(2,1)} copy(bf16[1,896,1024]{1,2,0:T(8,128)(2,1)} %get-tuple-element.27) | data formatting | bytes 3670016
  342.8 0.0 copy-done.2
  342.8 2.4 copy.40
  (12 shorter events, 0.1 us)
Async XLA Ops:
  7.2 4.9 %copy-start.4 = (bf16[128,1024]{1,0:T(8,128)(2,1)S(1)}, bf16[128,1024]{1,0:T(8,128)(2,1)}, u32[]{:S(2)}) copy-start(bf16[128,1024]{1,0:T(8,128)(2,1)} %param.10) | copy-start | bytes 786436
  13.4 36.9 %all-to-all-start = ((bf16[4,128,1280]{2,1,0:T(8,128)(2,1)}), bf16[4,128,1280]{2,1,0:T(8,128)(2,1)S(1)}, u32[]{:S(2)}, u32[]{:S(2)}) async-start(bf16[4,128,1280]{2,1,0:T(8,128)(2,1)} %pad_maximum_fusion.3), calls=%async_computation | async-start | bytes 2621440 | tf_op jit(solution)/shard_map/all_to_all | solution.py:69
  60.5 98.5 %all-to-all-start.1 = ((bf16[64,24,1152]{2,1,0:T(8,128)(2,1)}), bf16[64,24,1152]{2,1,0:T(8,128)(2,1)}, u32[]{:S(2)}, u32[]{:S(2)}) async-start(bf16[64,24,1152]{2,1,0:T(8,128)(2,1)} %bitcast.47), calls=%async_computation.1 | async-start | bytes 7077888 | tf_op jit(solution)/shard_map/all_to_all | solution.py:88
  74.9 6.1 %copy-start.6 = (s32[64]{0:T(128)S(1)}, s32[64]{0:T(128)}, u32[]{:S(2)}) copy-start(s32[64]{0:T(128)} %param.14) | copy-start | bytes 772
  74.9 162.3 %reduce-scatter.2.cloned.1.call-start = ((), (), s32[]{:S(2)}) async-start(), calls=%async_computation.3 | async-start | bytes 3932160 | tf_op jit(solution)/shard_map/reduce_scatter | solution.py:102
  78.0 78.0 %collective-permute-start = (bf16[1,896,1024]{1,2,0:T(8,128)(2,1)S(1)}, bf16[1,896,1024]{1,2,0:T(8,128)(2,1)}, u32[]{:S(2)}, u32[]{:S(2)}) collective-permute-start(bf16[1,896,1024]{1,2,0:T(8,128)(2,1)S(1)} %copy.26), channel_id=1, source_target_pairs={{0,32},{1,33},{2,34},{3,35},{4,36},{5,37},{6,38},{7,39},{8,40},{9,... | collective-permute-start | bytes 5505032 | tf_op jit(solution)/shard_map/ppermute | solution.py:19
  158.9 3.0 copy-start.3
  172.2 129.2 %all-gather.3.cloned.1.call-start = ((), (), s32[]{:S(2)}) async-start(), calls=%async_computation.4 | async-start | bytes 3932160 | tf_op jit(solution)/shard_map/all_gather | solution.py:105
  244.0 69.3 %collective-permute-start.1 = (bf16[1,896,1024]{1,2,0:T(8,128)(2,1)}, bf16[1,896,1024]{1,2,0:T(8,128)(2,1)}, u32[]{:S(2)}, u32[]{:S(2)}) collective-permute-start(bf16[1,896,1024]{1,2,0:T(8,128)(2,1)} %copy.28), channel_id=1, source_target_pairs={{0,32},{1,33},{2,34},{3,35},{4,36},{5,37},{6,38},{7,39},{8,40},{9,... | collective-permute-start | bytes 5505032 | tf_op jit(solution)/shard_map/ppermute | solution.py:19
  250.5 75.5 %collective-permute-start.2 = (bf16[1,896,1024]{1,2,0:T(8,128)(2,1)}, bf16[1,896,1024]{1,2,0:T(8,128)(2,1)}, u32[]{:S(2)}, u32[]{:S(2)}) collective-permute-start(bf16[1,896,1024]{1,2,0:T(8,128)(2,1)} %copy.36), channel_id=1, source_target_pairs={{0,32},{1,33},{2,34},{3,35},{4,36},{5,37},{6,38},{7,39},{8,40},{9,... | collective-permute-start | bytes 5505032 | tf_op jit(solution)/shard_map/ppermute | solution.py:19
  301.5 3.1 copy-start.5
  310.3 15.8 %copy-start = (bf16[1,896,1024]{1,2,0:T(8,128)(2,1)S(1)}, bf16[1,896,1024]{1,2,0:T(8,128)(2,1)}, u32[]{:S(2)}) copy-start(bf16[1,896,1024]{1,2,0:T(8,128)(2,1)} %copy.28) | copy-start | bytes 5505028
  310.3 15.8 %copy-start.1 = (bf16[1,896,1024]{1,2,0:T(8,128)(2,1)S(1)}, bf16[1,896,1024]{1,2,0:T(8,128)(2,1)}, u32[]{:S(2)}) copy-start(bf16[1,896,1024]{1,2,0:T(8,128)(2,1)} %copy.36) | copy-start | bytes 5505028
  338.9 3.9 %copy-start.2 = (bf16[1,896,1024]{1,2,0:T(8,128)(2,1)S(1)}, bf16[1,896,1024]{1,2,0:T(8,128)(2,1)}, u32[]{:S(2)}) copy-start(bf16[1,896,1024]{1,2,0:T(8,128)(2,1)} %get-tuple-element.25) | copy-start | bytes 5505028
Sparse Core Ops, SparseCore 0:
  172.4 64.8 reduce-scatter.1
  240.3 61.1 all-gather.2
